TPU v7x, 512 devices: a whole 4x4x16 slice. The times are simulated.
512 devices in a mesh: dp: 4 (over x_lo, core), expert: 128 (over y, x_hi, z).
Axes of the slice: x: 4 (x_hi: 2, x_lo: 2; x = x_hi * 2 + x_lo), y: 4, z: 16, core: 2. Of those that a mesh axis runs over, the one named last changes fastest.
Arguments:
- activations: bfloat16 [65536, 2048], P(('dp', 'expert')), may hold values from -6 to 6
- routed_experts: int32 [65536, 2], P(('dp', 'expert')), may hold values from 0 to 127, all different within a row; in each aligned block of 128 rows (0 to 127, 128 to 255, ...) at most 2 rows name the same one
- route_weights: float32 [65536, 2], P(('dp', 'expert')), may hold values from 0.25 to 1
- live_counts: int32 [4, 128], P('dp', 'expert'), may hold values from 32 to 128, as said below
- swap_partner: int32 [128], replicated, may hold values from 0 to 127, as said below
- gate_proj: bfloat16 [128, 2048, 768], P('expert', 'dp'), may hold values from -0.125 to 0.125
- up_proj: bfloat16 [128, 2048, 768], P('expert', 'dp'), may hold values from -0.125 to 0.125
- down_proj: bfloat16 [128, 2048, 768], P('expert', 'dp'), may hold values from -0.21875 to 0.21875
- first_moment: bfloat16 [128, 2048, 768], P('expert', 'dp'), may hold values from -6 to 6
- second_moment: bfloat16 [128, 2048], P('expert', 'dp'), may hold values from 0.5 to 20
Outputs:
- layer_output: bfloat16 [65536, 2048], P(('dp', 'expert'))
- update_direction: bfloat16 [128, 2048, 768], P('expert', 'dp')
Inputs may be any that keep to these rules, and one draw needn't show every extreme that they name: `routed_experts`: each token names 2 different experts; the 256 routed rows of one device name every expert exactly 2 times. The first live_counts tokens of a device's block are live, the rest are padding; some device has all 128 live. swap_partner[i] = i XOR p, where p is 64 or 32, the same for all i, so devices are swapped in pairs; expert i moves to device swap_partner[i].
All inputs are finite; a program needn't handle non-finite values.
Results may differ from a plain program's by a relative error of at most 0.015.
Values may be sent and summed in bfloat16 or wider, within the bound.
A program may use at most 64 MiB of HBM per device.

v0:
```python
from functools import partial

import jax
import jax.numpy as jnp
from jax import lax
from jax.sharding import PartitionSpec as P


def shortened(shard):
    return jax.tree.map(lambda a: a.astype(jnp.bfloat16) if a.dtype == jnp.float32 else a, shard)


def partner_2(block, axis, stride):
    count = lax.axis_size(axis)
    route = []
    for low in range(count):
        high = low | 1 << stride
        if high != low and high < count:
            route += [(low, high), (high, low)]
    return lax.ppermute(block, axis, route)


def move_state(stacked, shift_bit):
    return jax.tree.map(
        lambda part, own: part.astype(own.dtype),
        partner_2(shortened(stacked), "expert", shift_bit),
        stacked,
    )


def pair_select(mover, stacked, bit_place, levels):
    branches = [partial(mover, shift_bit=level_bit) for level_bit in range(levels - 2, levels)]
    return lax.switch(bit_place - (levels - 2), branches, stacked)


def local(
    activations,
    routed_experts,
    route_weights,
    live_counts,
    swap_partner,
    gate_proj,
    up_proj,
    down_proj,
    first_moment,
    second_moment,
):
    experts = swap_partner.shape[0]
    token_total, routes_per_token = routed_experts.shape
    model_width = activations.shape[1]
    hidden_width = gate_proj.shape[2]
    capacity = token_total * routes_per_token // experts
    levels = experts.bit_length() - 1
    partner = swap_partner[0]
    bit_place = jnp.int32(0)
    for level_bit in range(levels):
        bit_place = bit_place + jnp.where(partner == 1 << level_bit, level_bit, 0).astype(jnp.int32)
    ids_flat = routed_experts.reshape(-1)
    columns = jnp.arange(experts, dtype=jnp.int32)
    owners = jnp.sum(
        jnp.where(ids_flat[:, None] == columns[None, :], swap_partner[None, :], 0), axis=1
    )
    gate_local, up_local, down_local, first_local, second_local = pair_select(
        move_state, (gate_proj, up_proj, down_proj, first_moment, second_moment), bit_place, levels
    )
    matches = (owners[:, None] == columns[None, :]).astype(jnp.int32)
    slot_index = jnp.sum(matches * (jnp.cumsum(matches, axis=0) - 1), axis=1)
    routed_total = token_total * routes_per_token
    slot_rows = (
        jnp.zeros((experts, capacity), jnp.int32)
        .at[owners, slot_index]
        .set(jnp.arange(routed_total, dtype=jnp.int32))
    )
    slot_tokens = slot_rows // routes_per_token
    live_mask = (jnp.arange(token_total, dtype=jnp.int32) < live_counts[0, 0]).astype(jnp.float32)
    outgoing = activations[slot_tokens]
    arrived = lax.all_to_all(outgoing, "expert", split_axis=0, concat_axis=0, tiled=True)
    arrived_rows = arrived.reshape(experts * capacity, model_width)
    empty_sum = jnp.zeros((experts * capacity, hidden_width), jnp.float32)
    pieces_in = (
        lax.all_gather(shortened(gate_local), "dp", axis=1, tiled=True),
        lax.all_gather(shortened(up_local), "dp", axis=1, tiled=True),
    )
    column_block = lax.slice_in_dim(arrived_rows, 0, pieces_in[0].shape[1], axis=1)
    gate_part = jnp.dot(column_block, pieces_in[0][0], preferred_element_type=jnp.float32)
    up_part = jnp.dot(column_block, pieces_in[1][0], preferred_element_type=jnp.float32)
    gate_sum = empty_sum + gate_part
    up_sum = empty_sum + up_part
    hidden = (jax.nn.silu(gate_sum) * up_sum).astype(jnp.bfloat16)
    produced = jnp.einsum(
        "rf,nf->rn",
        hidden,
        lax.all_gather(shortened(down_local), "dp", axis=1, tiled=True)[0],
        preferred_element_type=jnp.float32,
    )
    produced = produced.astype(jnp.bfloat16).reshape(experts, capacity, model_width)
    returned = lax.all_to_all(produced, "expert", split_axis=0, concat_axis=0, tiled=True)
    picked = returned[owners, slot_index].reshape(token_total, routes_per_token, model_width)
    mixed_rows = jnp.zeros((token_total, model_width), jnp.float32)
    for choice_index in range(routes_per_token):
        mixed_rows = (
            mixed_rows
            + picked[:, choice_index].astype(jnp.float32) * route_weights[:, choice_index, None]
        )
    layer_output = (mixed_rows * live_mask[:, None]).astype(jnp.bfloat16)
    slot_weights = route_weights.reshape(-1)[slot_rows]
    sending = (slot_weights[:, :, None] * layer_output[slot_tokens].astype(jnp.float32)).astype(
        jnp.bfloat16
    )
    arrived_grad = lax.all_to_all(
        sending, "expert", split_axis=0, concat_axis=0, tiled=True
    ).reshape(experts * capacity, model_width)
    column_block = lax.slice_in_dim(
        arrived_grad, 0, gate_local.shape[1] * lax.axis_size("dp"), axis=1
    )
    grad_local = lax.psum_scatter(
        jnp.einsum("rd,rf->df", column_block, hidden, preferred_element_type=jnp.float32).astype(
            jnp.bfloat16
        ),
        "dp",
        scatter_dimension=0,
        tiled=True,
    ).astype(jnp.float32)
    first_new = 0.9 * first_local[0].astype(jnp.float32) + 0.1 * grad_local
    second_new = 0.99 * second_local[0].astype(jnp.float32) + 0.01 * jnp.mean(
        grad_local * grad_local, axis=1
    )
    update_direction = (first_new / (jnp.sqrt(second_new)[:, None] + 1e-08)).astype(jnp.bfloat16)[
        None
    ]
    return (layer_output, update_direction)


def solution(mesh):
    in_specs = (
        P(("dp", "expert"), None),
        P(("dp", "expert"), None),
        P(("dp", "expert"), None),
        P("dp", "expert"),
        P(),
        P("expert", "dp", None),
        P("expert", "dp", None),
        P("expert", "dp", None),
        P("expert", "dp", None),
        P("expert", "dp"),
    )
    out_specs = (P(("dp", "expert"), None), P("expert", "dp", None))
    return jax.shard_map(local, mesh=mesh, in_specs=in_specs, out_specs=out_specs, check_vma=False)
```

profile of v0, /device:TPU:1, one launch (start us, length us, event | category | flops | bytes accessed | tf_op | source)
XLA Modules:
  0.0 443.9 jit_solution(6263515358429149419)
XLA Ops:
  11.2 68.5 %conditional.3 = (bf16[1,512,768]{2,1,0:T(8,128)(2,1)}, bf16[1,512,768]{2,1,0:T(8,128)(2,1)}, bf16[1,512,768]{2,1,0:T(8,128)(2,1)}, f32[512,768]{1,0:T(8,128)}, f32[512,1]{0,1:T(1,128)S(1)}) conditional(s32[]{:T(128)} %bitcast.11, (bf16[1,512,768]{2,1,0:T(8,128)(2,1)}, bf16[1,512,768]{2,1,0:T(8,128)(2,1)}, bf16[1,512,768]{2,1,0:T(8,128)(2,1)}, ...), branch_computations={%region_5.6_spmd, %region_6.7_spmd} | conditional | flops 393728 | bytes 14949616
  11.2 4.0 collective-permute-start.3
  17.2 3.4 collective-permute-start.1
  20.6 1.9 collective-permute-start.2
  22.5 3.4 collective-permute-start.4
  25.9 52.6 %collective-permute-done.4 = bf16[1,512]{1,0:T(2,128)(2,1)S(1)} collective-permute-done((bf16[1,512]{1,0:T(2,128)(2,1)}, bf16[1,512]{1,0:T(2,128)(2,1)S(1)}, u32[]{:S(2)}, u32[]{:S(2)}) %collective-permute-start.4) | collective-permute-done | bytes 1056 | tf_op jit(solution)/shard_map/cond/branch_0_fun/ppermute | solution.py:20
  81.6 11.1 %scatter_fusion = s32[128,2]{0,1:T(2,128)S(1)} fusion(s32[128,2]{0,1:T(2,128)S(1)} %broadcast.92, s32[256]{0:T(256)S(1)} %bitcast.68, s32[256]{0:T(256)S(1)} %iota.16), kind=kCustom, calls=%fused_computation.4 | custom fusion | bytes 5120 | tf_op jit(solution)/shard_map/scatter | solution.py:72
  95.9 26.9 %all-to-all-start = ((bf16[128,2,2048]{2,1,0:T(2,128)(2,1)}), bf16[128,2,2048]{2,1,0:T(2,128)(2,1)S(1)}, u32[]{:S(2)}, u32[]{:S(2)}) async-start(bf16[128,2,2048]{2,1,0:T(2,128)(2,1)} %reshape.150), calls=%async_computation | async-start | bytes 2097152 | tf_op jit(solution)/shard_map/all_to_all | solution.py:77
  123.6 48.7 %all-to-all-done = bf16[128,2,2048]{2,1,0:T(2,128)(2,1)S(1)} async-done(((bf16[128,2,2048]{2,1,0:T(2,128)(2,1)}), bf16[128,2,2048]{2,1,0:T(2,128)(2,1)S(1)}, u32[]{:S(2)}, u32[]{:S(2)}) %all-to-all-start) | async-done | bytes 1048608 | tf_op jit(solution)/shard_map/all_to_all | solution.py:77
  172.8 2.9 fusion.4
  175.7 15.6 %all-gather.6.cloned.1.call-done = bf16[1,2048,768]{2,1,0:T(8,128)(2,1)} async-done(((bf16[1,512,768]{2,1,0:T(8,128)(2,1)}), bf16[1,2048,768]{2,1,0:T(8,128)(2,1)}) %all-gather.6.cloned.1.call-update) | async-done | bytes 3145744 | tf_op jit(solution)/shard_map/all_gather | solution.py:82
  191.3 2.9 fusion.16
  194.3 45.0 %all-gather.8.cloned.1.call-done = bf16[1,2048,768]{2,1,0:T(8,128)(2,1)} async-done(((bf16[1,512,768]{2,1,0:T(8,128)(2,1)}), bf16[1,2048,768]{2,1,0:T(8,128)(2,1)}) %all-gather.8.cloned.1.call-update) | async-done | bytes 3145744 | tf_op jit(solution)/shard_map/all_gather | solution.py:93
  239.2 2.9 fusion.6
  243.7 18.7 %all-to-all-start.1 = ((bf16[128,2,2048]{2,1,0:T(2,128)(2,1)}), bf16[128,2,2048]{2,1,0:T(2,128)(2,1)S(1)}, u32[]{:S(2)}, u32[]{:S(2)}) async-start(bf16[128,2,2048]{2,1,0:T(2,128)(2,1)} %reshape.134), calls=%async_computation.1 | async-start | bytes 2097152 | tf_op jit(solution)/shard_map/all_to_all | solution.py:97
  263.8 1.9 gather_fusion.2
  266.5 47.4 %all-to-all-done.1 = bf16[128,2,2048]{2,1,0:T(2,128)(2,1)S(1)} async-done(((bf16[128,2,2048]{2,1,0:T(2,128)(2,1)}), bf16[128,2,2048]{2,1,0:T(2,128)(2,1)S(1)}, u32[]{:S(2)}, u32[]{:S(2)}) %all-to-all-start.1) | async-done | bytes 1048608 | tf_op jit(solution)/shard_map/all_to_all | solution.py:97
  313.9 3.0 gather_fusion.1
  319.8 2.3 gather_fusion.3
  322.1 2.4 reshape.194
  326.2 62.9 %all_to_all.15 = bf16[128,2,2048]{2,1,0:T(2,128)(2,1)S(1)} all-to-all(bf16[128,2,2048]{2,1,0:T(2,128)(2,1)S(1)} %multiply_convert_fusion), channel_id=1, replica_groups=mesh['dp'=4,'expert'=128] {'expert'}, dimensions={0} | all-to-all | bytes 2097152 | tf_op jit(solution)/shard_map/all_to_all | solution.py:110
  389.5 2.7 convolution_convert_fusion
  392.2 41.0 %reduce-scatter.2.cloned.1.call-done = bf16[512,768]{1,0:T(8,128)(2,1)} async-done(((bf16[2048,768]{1,0:T(8,128)(2,1)}), bf16[512,768]{1,0:T(8,128)(2,1)}) %reduce-scatter.2.cloned.1.call-update) | async-done | bytes 786448 | tf_op jit(solution)/shard_map/reduce_scatter | solution.py:116
  434.6 2.8 fusion.22
  (64 shorter events, 18.7 us)
Async XLA Ops:
  7.2 85.8 %copy-start = (bf16[128,2048]{1,0:T(8,128)(2,1)S(1)}, bf16[128,2048]{1,0:T(8,128)(2,1)}, u32[]{:S(2)}) copy-start(bf16[128,2048]{1,0:T(8,128)(2,1)} %param.12) | copy-start | bytes 1572868
  7.2 165.6 %all-gather.4.cloned.1.call-start = ((), (), s32[]{:S(2)}) async-start(), calls=%async_computation.4 | async-start | bytes 3932160 | tf_op jit(solution)/shard_map/all_gather | solution.py:81
  11.2 69.3 %copy-start.3 = (s32[128,2]{0,1:T(2,128)S(1)}, s32[128,2]{0,1:T(2,128)}, u32[]{:S(2)}) copy-start(s32[128,2]{0,1:T(2,128)} %param.13) | copy-start | bytes 3076
  11.2 69.6 %copy-start.4 = (s32[128]{0:T(128)S(1)}, s32[128]{0:T(128)}, u32[]{:S(2)}) copy-start(s32[128]{0:T(128)} %param.16) | copy-start | bytes 1540
  11.2 67.3 %collective-permute-start.3 = (bf16[1,512,768]{2,1,0:T(8,128)(2,1)}, bf16[1,512,768]{2,1,0:T(8,128)(2,1)S(1)}, u32[]{:S(2)}, u32[]{:S(2)}) collective-permute-start(bf16[1,512,768]{2,1,0:T(8,128)(2,1)} %get-tuple-element.41), channel_id=1, source_target_pairs={{0,32},{32,0},{1,33},{33,1},{2,34},{34,2},{3,35},{35,3},{4,36},{36... | collective-permute-start | bytes 2359304 | tf_op jit(solution)/shard_map/cond/branch_0_fun/ppermute | solution.py:20
  15.2 64.5 %collective-permute-start = (bf16[1,512,768]{2,1,0:T(8,128)(2,1)}, bf16[1,512,768]{2,1,0:T(8,128)(2,1)}, u32[]{:S(2)}, u32[]{:S(2)}) collective-permute-start(bf16[1,512,768]{2,1,0:T(8,128)(2,1)} %get-tuple-element.38), channel_id=1, source_target_pairs={{0,32},{32,0},{1,33},{33,1},{2,34},{34,2},{3,35},{35,3},{4,36},{36... | collective-permute-start | bytes 2359304 | tf_op jit(solution)/shard_map/cond/branch_0_fun/ppermute | solution.py:20
  17.2 62.5 %collective-permute-start.1 = (bf16[1,512,768]{2,1,0:T(8,128)(2,1)}, bf16[1,512,768]{2,1,0:T(8,128)(2,1)}, u32[]{:S(2)}, u32[]{:S(2)}) collective-permute-start(bf16[1,512,768]{2,1,0:T(8,128)(2,1)} %get-tuple-element.39), channel_id=1, source_target_pairs={{0,32},{32,0},{1,33},{33,1},{2,34},{34,2},{3,35},{35,3},{4,36},{36... | collective-permute-start | bytes 2359304 | tf_op jit(solution)/shard_map/cond/branch_0_fun/ppermute | solution.py:20
  20.6 59.2 %collective-permute-start.2 = (bf16[1,512,768]{2,1,0:T(8,128)(2,1)}, bf16[1,512,768]{2,1,0:T(8,128)(2,1)}, u32[]{:S(2)}, u32[]{:S(2)}) collective-permute-start(bf16[1,512,768]{2,1,0:T(8,128)(2,1)} %get-tuple-element.40), channel_id=1, source_target_pairs={{0,32},{32,0},{1,33},{33,1},{2,34},{34,2},{3,35},{35,3},{4,36},{36... | collective-permute-start | bytes 2359304 | tf_op jit(solution)/shard_map/cond/branch_0_fun/ppermute | solution.py:20
  22.5 56.0 %collective-permute-start.4 = (bf16[1,512]{1,0:T(2,128)(2,1)}, bf16[1,512]{1,0:T(2,128)(2,1)S(1)}, u32[]{:S(2)}, u32[]{:S(2)}) collective-permute-start(bf16[1,512]{1,0:T(2,128)(2,1)} %get-tuple-element.42), channel_id=1, source_target_pairs={{0,32},{32,0},{1,33},{33,1},{2,34},{34,2},{3,35},{35,3},{4,36},{36... | collective-permute-start | bytes 3080 | tf_op jit(solution)/shard_map/cond/branch_0_fun/ppermute | solution.py:20
  79.7 111.6 %all-gather.6.cloned.1.call-start = ((), (), s32[]{:S(2)}) async-start(), calls=%async_computation.5 | async-start | bytes 3932160 | tf_op jit(solution)/shard_map/all_gather | solution.py:82
  95.9 76.4 %all-to-all-start = ((bf16[128,2,2048]{2,1,0:T(2,128)(2,1)}), bf16[128,2,2048]{2,1,0:T(2,128)(2,1)S(1)}, u32[]{:S(2)}, u32[]{:S(2)}) async-start(bf16[128,2,2048]{2,1,0:T(2,128)(2,1)} %reshape.150), calls=%async_computation | async-start | bytes 2097152 | tf_op jit(solution)/shard_map/all_to_all | solution.py:77
  122.8 116.4 %all-gather.8.cloned.1.call-start = ((), (), s32[]{:S(2)}) async-start(), calls=%async_computation.6 | async-start | bytes 3932160 | tf_op jit(solution)/shard_map/all_gather | solution.py:93
  242.1 21.4 %copy-start.2 = (f32[128,2]{0,1:T(2,128)S(1)}, f32[128,2]{0,1:T(2,128)}, u32[]{:S(2)}) copy-start(f32[128,2]{0,1:T(2,128)} %param.14) | copy-start | bytes 3076
  243.7 70.2 %all-to-all-start.1 = ((bf16[128,2,2048]{2,1,0:T(2,128)(2,1)}), bf16[128,2,2048]{2,1,0:T(2,128)(2,1)S(1)}, u32[]{:S(2)}, u32[]{:S(2)}) async-start(bf16[128,2,2048]{2,1,0:T(2,128)(2,1)} %reshape.134), calls=%async_computation.1 | async-start | bytes 2097152 | tf_op jit(solution)/shard_map/all_to_all | solution.py:97
  262.4 170.8 %reduce-scatter.2.cloned.1.call-start = ((), (), s32[]{:S(2)}) async-start(), calls=%async_computation.7 | async-start | bytes 3932160 | tf_op jit(solution)/shard_map/reduce_scatter | solution.py:116
  319.8 2.4 copy-start.1
Sparse Core Ops, SparseCore 0:
  79.9 60.0 all-gather.3
  142.0 49.2 all-gather.5
  193.4 45.7 all-gather.7
  392.3 40.8 reduce-scatter.1
where the time goes:
time: 445 us; the launch traced here: 444 us
  waiting for transfers between devices  252 us (57%)
  blocking collectives  62.9 us (14%)
  starting transfers between devices  60.6 us (14%)
  local copies, waits for them, and re-layouts  30.1 us (7%)
  between operations  18.7 us (4%)
  matrix products  11.5 us (3%)
  other arithmetic  8.48 us (2%)
    all_to_all x1, blocking collectives, local(): lax.all_to_all(sending, 'expert', split_axis=0, concat_axis=0, tiled=True)  62.9 us
    ppermute x5, waiting for transfers between devices, partner_2(): return lax.ppermute(block, axis, route)  52.6 us
    all_to_all x1, waiting for transfers between devices, local(): lax.all_to_all(outgoing, 'expert', split_axis=0, concat_axis=0, tiled=True)  48.7 us
    all_to_all x1, waiting for transfers between devices, local(): lax.all_to_all(produced, 'expert', split_axis=0, concat_axis=0, tiled=True)  47.4 us
    all_gather x1, waiting for transfers between devices, local(): lax.all_gather(shortened(down_local), 'dp', axis=1, tiled=True)[0]  45 us
    reduce_scatter x1, waiting for transfers between devices, local(): lax.psum_scatter(jnp.einsum('rd,rf->df', column_block, hidden, preferred_...  41 us
    all_to_all x1, starting transfers between devices, local(): lax.all_to_all(outgoing, 'expert', split_axis=0, concat_axis=0, tiled=True)  26.9 us
    all_to_all x1, starting transfers between devices, local(): lax.all_to_all(produced, 'expert', split_axis=0, concat_axis=0, tiled=True)  18.7 us
  transfers between devices with their start and end apart: 11, of which 6 were waited for; matrix products, arithmetic and copies ran while one was open for 6% of the time, Pallas kernels for 0%

commit v1 on v0

v1 whole, which is shorter than its diff:
```python
import jax
import jax.numpy as jnp
from jax import lax
from jax.sharding import PartitionSpec as P

F32 = jnp.float32
BF16 = jnp.bfloat16


def exchange(block, axis, distance):
    count = lax.axis_size(axis)
    return lax.ppermute(block, axis, [(i, i ^ distance) for i in range(count)])


def dot(a, b):
    return jnp.dot(a, b, preferred_element_type=F32)


def slot_table(ids, experts, capacity):
    tokens = ids.shape[0]
    slot = lax.broadcasted_iota(jnp.int32, (experts * capacity, tokens), 0)
    named = slot // capacity
    match = (named == ids[:, 0][None, :]) | (named == ids[:, 1][None, :])
    earlier = (
        lax.broadcasted_iota(jnp.int32, (tokens, tokens), 0)
        < lax.broadcasted_iota(jnp.int32, (tokens, tokens), 1)
    ).astype(BF16)
    rank = dot(match.astype(BF16), earlier)
    return match & (rank == (slot % capacity).astype(F32)), named


def local(
    activations,
    routed_experts,
    route_weights,
    live_counts,
    swap_partner,
    gate_proj,
    up_proj,
    down_proj,
    first_moment,
    second_moment,
):
    experts = swap_partner.shape[0]
    tokens, choices = routed_experts.shape
    width = activations.shape[1]
    capacity = tokens * choices // experts
    rows = experts * capacity
    part = gate_proj.shape[1]
    groups = lax.axis_size("dp")
    q = lax.axis_index("dp")
    partner = swap_partner[0]
    far, near = experts // 2, experts // 4

    def to_experts(block):
        block = block.reshape(experts, capacity, width)
        out = lax.all_to_all(block, "expert", split_axis=0, concat_axis=0, tiled=True)
        return out.reshape(rows, width)

    def moved(block):
        return jnp.where(
            partner == far, exchange(block, "expert", far), exchange(block, "expert", near)
        )

    def shards(weight):
        own = weight[0]
        across = exchange(own, "dp", 2)
        return own, exchange(own, "dp", 1), across, exchange(across, "dp", 1)

    place, named = slot_table(routed_experts, experts, capacity)
    outgoing = dot(place.astype(BF16), activations).astype(BF16)
    arrived = to_experts(outgoing)
    gates, ups, downs = shards(gate_proj), shards(up_proj), shards(down_proj)
    first_here = moved(first_moment[0])
    second_here = moved(second_moment[0])

    gate_sum = jnp.zeros((rows, gate_proj.shape[2]), F32)
    up_sum = gate_sum
    for m in range(groups):
        columns = lax.dynamic_slice_in_dim(arrived, (q ^ m) * part, part, axis=1)
        gate_sum = gate_sum + dot(columns, gates[m])
        up_sum = up_sum + dot(columns, ups[m])
    hidden = (jax.nn.silu(gate_sum) * up_sum).astype(BF16)
    produced = jnp.stack(
        [
            jnp.einsum("rf,nf->rn", hidden, downs[m], preferred_element_type=F32).astype(BF16)
            for m in range(groups)
        ]
    )
    produced = jnp.concatenate(
        [lax.dynamic_index_in_dim(produced, q ^ b, 0, keepdims=False) for b in range(groups)],
        axis=1,
    )
    returned = to_experts(produced)
    hidden_here = lax.all_gather(moved(hidden), "dp", axis=0, tiled=True)

    total = jnp.zeros((tokens, width), F32)
    for k in range(choices):
        pick = (place & (named == routed_experts[:, k][None, :])).astype(BF16)
        picked = lax.dot_general(
            pick, returned, (((0,), (0,)), ((), ())), preferred_element_type=F32
        )
        total = total + picked * route_weights[:, k, None]
    live = (jnp.arange(tokens, dtype=jnp.int32) < live_counts[0, 0]).astype(F32)
    layer_output = (total * live[:, None]).astype(BF16)

    new_place, new_named = slot_table(routed_experts ^ partner, experts, capacity)
    first_choice = new_named == (routed_experts[:, 0] ^ partner)[None, :]
    slot_weight = jnp.sum(
        jnp.where(
            new_place,
            jnp.where(first_choice, route_weights[:, 0][None, :], route_weights[:, 1][None, :]),
            0.0,
        ),
        axis=1,
        keepdims=True,
    )
    cotangent = (slot_weight * dot(new_place.astype(BF16), layer_output)).astype(BF16)
    cotangent = to_experts(cotangent)
    own_part = lax.all_to_all(cotangent, "dp", split_axis=1, concat_axis=0, tiled=True)
    gradient = lax.dot_general(
        own_part, hidden_here, (((0,), (0,)), ((), ())), preferred_element_type=F32
    )
    first_new = 0.9 * first_here.astype(F32) + 0.1 * gradient
    second_new = 0.99 * second_here.astype(F32) + 0.01 * jnp.mean(gradient * gradient, axis=1)
    update = (first_new / (jnp.sqrt(second_new)[:, None] + 1e-08)).astype(BF16)
    return layer_output, update[None]


def solution(mesh):
    in_specs = (
        P(("dp", "expert"), None),
        P(("dp", "expert"), None),
        P(("dp", "expert"), None),
        P("dp", "expert"),
        P(),
        P("expert", "dp", None),
        P("expert", "dp", None),
        P("expert", "dp", None),
        P("expert", "dp", None),
        P("expert", "dp"),
    )
    out_specs = (P(("dp", "expert"), None), P("expert", "dp", None))
    return jax.shard_map(local, mesh=mesh, in_specs=in_specs, out_specs=out_specs, check_vma=False)
```

time: 445 us -> 315 us (0.71)
  waiting for transfers between devices: 252 us -> 160 us
  blocking collectives: 62.9 us -> 0 us
  starting transfers between devices: 60.6 us -> 108 us
  local copies, waits for them, and re-layouts: 30.1 us -> 7.05 us
  matrix products: 11.5 us -> 18.5 us
    all_to_all x1 -> x0, blocking collectives: 62.9 us -> none  [local(): lax.all_to_all(sending, 'expert', split_axis=0, concat_axis=0, tiled=True)]
    all_gather x3 -> x1, waiting for transfers between devices: 60.6 us -> 0.02 us  [local(): hidden_here = lax.all_gather(moved(hidden), 'dp', axis=0, tiled=True)]
    reduce_scatter x1 -> x0, waiting for transfers between devices: 41 us -> none  [local(): lax.psum_scatter(jnp.einsum('rd,rf->df', column_block, hidden, preferred_...]
    ppermute x5 -> x15, starting transfers between devices: 14.6 us -> 45.6 us  [exchange(): return lax.ppermute(block, axis, [(i, i ^ distance) for i in range(count)])]
    all_to_all x2 -> x4, starting transfers between devices: 45.6 us -> 61.9 us  [the longest x3 53.8 us: to_experts(): lax.all_to_all(block, 'expert', split_axis=0, concat_axis=0, tiled=True)]
    all_to_all x2 -> x4, waiting for transfers between devices: 96.1 us -> 112 us  [the longest x3 110 us: to_experts(): lax.all_to_all(block, 'expert', split_axis=0, concat_axis=0, tiled=True)]
    scatter x1 -> x0, local copies, waits for them, and re-layouts: 11.1 us -> none  [local(): slot_rows = jnp.zeros((experts, capacity), jnp.int32).at[owners, slot_ind...]
    gather x6 -> x0, local copies, waits for them, and re-layouts: 10.9 us -> none  [the longest x1 2.96 us: local(): returned[owners, slot_index]]
  transfers between devices with their start and end apart: 11 -> 20, of which waited for: 6 -> 9; matrix products, arithmetic and copies ran while one was open for 6% -> 6% of each run, Pallas kernels for 0% -> 0%
where the time goes in v1:
time: 315 us; the launch traced here: 312 us
  waiting for transfers between devices  160 us (51%)
  starting transfers between devices  108 us (34%)
  matrix products  18.5 us (6%)
  between operations  15.3 us (5%)
  local copies, waits for them, and re-layouts  7.05 us (2%)
  other arithmetic  4.17 us (1%)
    all_to_all x3, waiting for transfers between devices, to_experts(): lax.all_to_all(block, 'expert', split_axis=0, concat_axis=0, tiled=True)  110 us
    all_to_all x3, starting transfers between devices, to_experts(): lax.all_to_all(block, 'expert', split_axis=0, concat_axis=0, tiled=True)  53.8 us
    ppermute x15, waiting for transfers between devices, exchange(): return lax.ppermute(block, axis, [(i, i ^ distance) for i in range(count)])  47.9 us
    ppermute x15, starting transfers between devices, exchange(): return lax.ppermute(block, axis, [(i, i ^ distance) for i in range(count)])  45.6 us
    dot_general x12, matrix products, dot(): return jnp.dot(a, b, preferred_element_type=F32)  11.1 us
    all_to_all x1, starting transfers between devices, local(): lax.all_to_all(cotangent, 'dp', split_axis=1, concat_axis=0, tiled=True)  8.1 us
  transfers between devices with their start and end apart: 20, of which 9 were waited for; matrix products, arithmetic and copies ran while one was open for 6% of the time, Pallas kernels for 0%

profile of v1, /device:TPU:1, one launch (start us, length us, event | category | flops | bytes accessed | tf_op | source)
XLA Modules:
  0.0 312.3 jit_solution(15979521067353895274)
XLA Ops:
  10.6 23.1 %all-to-all-start = ((bf16[128,2,2048]{2,1,0:T(2,128)(2,1)}), bf16[128,2,2048]{2,1,0:T(2,128)(2,1)S(1)}, u32[]{:S(2)}, u32[]{:S(2)}) async-start(bf16[128,2,2048]{2,1,0:T(2,128)(2,1)} %reshape.49), calls=%async_computation | async-start | bytes 2097152 | tf_op jit(solution)/shard_map/all_to_all | solution.py:57
  33.8 2.9 collective-permute-start
  38.9 3.1 collective-permute-start.4
  41.9 2.2 collective-permute-start.7
  44.2 2.8 collective-permute-start.3
  47.0 37.0 %all-to-all-done = bf16[128,2,2048]{2,1,0:T(2,128)(2,1)S(1)} async-done(((bf16[128,2,2048]{2,1,0:T(2,128)(2,1)}), bf16[128,2,2048]{2,1,0:T(2,128)(2,1)S(1)}, u32[]{:S(2)}, u32[]{:S(2)}) %all-to-all-start) | async-done | bytes 1048608 | tf_op jit(solution)/shard_map/all_to_all | solution.py:57
  84.8 6.7 %collective-permute-start.6 = (bf16[512,768]{1,0:T(8,128)(2,1)}, bf16[512,768]{1,0:T(8,128)(2,1)S(1)}, u32[]{:S(2)}, u32[]{:S(2)}) collective-permute-start(bf16[512,768]{1,0:T(8,128)(2,1)} %bitcast.4), channel_id=1, source_target_pairs={{0,128},{128,0},{256,384},{384,256},{1,129},{129,1},{257,385},{385... | collective-permute-start | bytes 2359304 | tf_op jit(solution)/shard_map/ppermute | solution.py:12
  93.4 2.4 collective-permute-start.5
  95.8 5.5 %collective-permute-done.7 = bf16[512,768]{1,0:T(8,128)(2,1)} collective-permute-done((bf16[512,768]{1,0:T(8,128)(2,1)}, bf16[512,768]{1,0:T(8,128)(2,1)}, u32[]{:S(2)}, u32[]{:S(2)}) %collective-permute-start.7) | collective-permute-done | bytes 786464 | tf_op jit(solution)/shard_map/ppermute | solution.py:12
  101.3 2.6 collective-permute-start.8
  118.8 17.7 %all-to-all-start.1 = ((bf16[128,2,2048]{2,1,0:T(2,128)(2,1)}), bf16[128,2,2048]{2,1,0:T(2,128)(2,1)S(1)}, u32[]{:S(2)}, u32[]{:S(2)}) async-start(bf16[128,2,2048]{2,1,0:T(2,128)(2,1)} %pad_maximum_fusion.1), calls=%async_computation.1 | async-start | bytes 2097152 | tf_op jit(solution)/shard_map/all_to_all | solution.py:57
  138.1 49.4 %all-to-all-done.1 = bf16[128,2,2048]{2,1,0:T(2,128)(2,1)S(1)} async-done(((bf16[128,2,2048]{2,1,0:T(2,128)(2,1)}), bf16[128,2,2048]{2,1,0:T(2,128)(2,1)S(1)}, u32[]{:S(2)}, u32[]{:S(2)}) %all-to-all-start.1) | async-done | bytes 1048608 | tf_op jit(solution)/shard_map/all_to_all | solution.py:57
  190.9 13.0 %all-to-all-start.2 = ((bf16[128,2,2048]{2,1,0:T(2,128)(2,1)}), bf16[128,2,2048]{2,1,0:T(2,128)(2,1)S(1)}, u32[]{:S(2)}, u32[]{:S(2)}) async-start(bf16[128,2,2048]{2,1,0:T(2,128)(2,1)} %reshape.52), calls=%async_computation.2 | async-start | bytes 2097152 | tf_op jit(solution)/shard_map/all_to_all | solution.py:57
  204.0 4.3 %collective-permute-start.11 = (bf16[256,768]{1,0:T(8,128)(2,1)S(1)}, bf16[256,768]{1,0:T(8,128)(2,1)S(1)}, u32[]{:S(2)}, u32[]{:S(2)}) collective-permute-start(bf16[256,768]{1,0:T(8,128)(2,1)S(1)} %multiply_convert_fusion), channel_id=1, source_target_pairs={{0,64},{1,65},{2,66},{3,67},{4,68},{5,69},{6,70},{7,71},{8,72},{9,... | collective-permute-start | bytes 1179656 | tf_op jit(solution)/shard_map/ppermute | solution.py:12
  208.3 2.4 collective-permute-start.12
  210.7 8.5 %collective-permute-done.11 = bf16[256,768]{1,0:T(8,128)(2,1)S(1)} collective-permute-done((bf16[256,768]{1,0:T(8,128)(2,1)S(1)}, bf16[256,768]{1,0:T(8,128)(2,1)S(1)}, u32[]{:S(2)}, u32[]{:S(2)}) %collective-permute-start.11) | collective-permute-done | bytes 393248 | tf_op jit(solution)/shard_map/ppermute | solution.py:12
  219.3 10.1 %collective-permute-done.12 = bf16[256,768]{1,0:T(8,128)(2,1)S(1)} collective-permute-done((bf16[256,768]{1,0:T(8,128)(2,1)S(1)}, bf16[256,768]{1,0:T(8,128)(2,1)S(1)}, u32[]{:S(2)}, u32[]{:S(2)}) %collective-permute-start.12) | collective-permute-done | bytes 393248 | tf_op jit(solution)/shard_map/ppermute | solution.py:12
  230.2 24.1 %all-to-all-done.2 = bf16[128,2,2048]{2,1,0:T(2,128)(2,1)S(1)} async-done(((bf16[128,2,2048]{2,1,0:T(2,128)(2,1)}), bf16[128,2,2048]{2,1,0:T(2,128)(2,1)S(1)}, u32[]{:S(2)}, u32[]{:S(2)}) %all-to-all-start.2) | async-done | bytes 1048608 | tf_op jit(solution)/shard_map/all_to_all | solution.py:57
  256.2 8.1 %all-to-all-start.3 = ((bf16[256,4,512]{2,0,1:T(8,128)(2,1)}), bf16[256,4,512]{2,0,1:T(8,128)(2,1)S(1)}, u32[]{:S(2)}, u32[]{:S(2)}) async-start(bf16[256,4,512]{2,0,1:T(8,128)(2,1)} %copy.17), calls=%async_computation.3 | async-start | bytes 2097152 | tf_op jit(solution)/shard_map/all_to_all | solution.py:120
  264.3 4.6 %collective-permute-start.9 = (bf16[512,768]{1,0:T(8,128)(2,1)}, bf16[512,768]{1,0:T(8,128)(2,1)S(1)}, u32[]{:S(2)}, u32[]{:S(2)}) collective-permute-start(bf16[512,768]{1,0:T(8,128)(2,1)} %bitcast.13), channel_id=1, source_target_pairs={{0,64},{1,65},{2,66},{3,67},{4,68},{5,69},{6,70},{7,71},{8,72},{9,... | collective-permute-start | bytes 2359304 | tf_op jit(solution)/shard_map/ppermute | solution.py:12
  268.9 2.4 collective-permute-start.10
  271.3 3.3 %collective-permute-start.13 = (bf16[512]{0:T(512)(128)(2,1)S(1)}, bf16[512]{0:T(512)(128)(2,1)S(1)}, u32[]{:S(2)}, u32[]{:S(2)}) collective-permute-start(bf16[512]{0:T(512)(128)(2,1)S(1)} %reduce), channel_id=1, source_target_pairs={{0,64},{1,65},{2,66},{3,67},{4,68},{5,69},{6,70},{7,71},{8,72},{9,... | collective-permute-start | bytes 3080 | tf_op jit(solution)/shard_map/ppermute | solution.py:12
  277.9 2.5 multiply_reduce_fusion
  280.4 23.2 %collective-permute-done.13 = bf16[512]{0:T(512)(128)(2,1)S(1)} collective-permute-done((bf16[512]{0:T(512)(128)(2,1)S(1)}, bf16[512]{0:T(512)(128)(2,1)S(1)}, u32[]{:S(2)}, u32[]{:S(2)}) %collective-permute-start.13) | collective-permute-done | bytes 1056 | tf_op jit(solution)/shard_map/ppermute | solution.py:12
  (77 shorter events, 35.3 us)
Async XLA Ops:
  10.6 23.1 %copy-start.2 = (bf16[1,512,768]{2,1,0:T(8,128)(2,1)S(1)}, bf16[1,512,768]{2,1,0:T(8,128)(2,1)}, u32[]{:S(2)}) copy-start(bf16[1,512,768]{2,1,0:T(8,128)(2,1)} %param.15) | copy-start | bytes 2359300
  10.6 73.3 %all-to-all-start = ((bf16[128,2,2048]{2,1,0:T(2,128)(2,1)}), bf16[128,2,2048]{2,1,0:T(2,128)(2,1)S(1)}, u32[]{:S(2)}, u32[]{:S(2)}) async-start(bf16[128,2,2048]{2,1,0:T(2,128)(2,1)} %reshape.49), calls=%async_computation | async-start | bytes 2097152 | tf_op jit(solution)/shard_map/all_to_all | solution.py:57
  33.8 51.0 %collective-permute-start = (bf16[512,768]{1,0:T(8,128)(2,1)S(1)}, bf16[512,768]{1,0:T(8,128)(2,1)}, u32[]{:S(2)}, u32[]{:S(2)}) collective-permute-start(bf16[512,768]{1,0:T(8,128)(2,1)S(1)} %bitcast.63), channel_id=1, source_target_pairs={{0,128},{128,0},{256,384},{384,256},{1,129},{129,1},{257,385},{385... | collective-permute-start | bytes 2359304 | tf_op jit(solution)/shard_map/ppermute | solution.py:12
  36.6 54.8 %collective-permute-start.1 = (bf16[512,768]{1,0:T(8,128)(2,1)S(1)}, bf16[512,768]{1,0:T(8,128)(2,1)}, u32[]{:S(2)}, u32[]{:S(2)}) collective-permute-start(bf16[512,768]{1,0:T(8,128)(2,1)S(1)} %bitcast.64), channel_id=1, source_target_pairs={{0,256},{128,384},{256,0},{384,128},{1,257},{129,385},{257,1},{385... | collective-permute-start | bytes 2359304 | tf_op jit(solution)/shard_map/ppermute | solution.py:12
  38.9 54.5 %collective-permute-start.4 = (bf16[512,768]{1,0:T(8,128)(2,1)}, bf16[512,768]{1,0:T(8,128)(2,1)}, u32[]{:S(2)}, u32[]{:S(2)}) collective-permute-start(bf16[512,768]{1,0:T(8,128)(2,1)} %bitcast.3), channel_id=1, source_target_pairs={{0,256},{128,384},{256,0},{384,128},{1,257},{129,385},{257,1},{385... | collective-permute-start | bytes 2359304 | tf_op jit(solution)/shard_map/ppermute | solution.py:12
  41.9 59.4 %collective-permute-start.7 = (bf16[512,768]{1,0:T(8,128)(2,1)}, bf16[512,768]{1,0:T(8,128)(2,1)}, u32[]{:S(2)}, u32[]{:S(2)}) collective-permute-start(bf16[512,768]{1,0:T(8,128)(2,1)} %bitcast.4), channel_id=1, source_target_pairs={{0,256},{128,384},{256,0},{384,128},{1,257},{129,385},{257,1},{385... | collective-permute-start | bytes 2359304 | tf_op jit(solution)/shard_map/ppermute | solution.py:12
  44.2 64.3 %collective-permute-start.3 = (bf16[512,768]{1,0:T(8,128)(2,1)}, bf16[512,768]{1,0:T(8,128)(2,1)}, u32[]{:S(2)}, u32[]{:S(2)}) collective-permute-start(bf16[512,768]{1,0:T(8,128)(2,1)} %bitcast.3), channel_id=1, source_target_pairs={{0,128},{128,0},{256,384},{384,256},{1,129},{129,1},{257,385},{385... | collective-permute-start | bytes 2359304 | tf_op jit(solution)/shard_map/ppermute | solution.py:12
  84.8 31.1 %collective-permute-start.6 = (bf16[512,768]{1,0:T(8,128)(2,1)}, bf16[512,768]{1,0:T(8,128)(2,1)S(1)}, u32[]{:S(2)}, u32[]{:S(2)}) collective-permute-start(bf16[512,768]{1,0:T(8,128)(2,1)} %bitcast.4), channel_id=1, source_target_pairs={{0,128},{128,0},{256,384},{384,256},{1,129},{129,1},{257,385},{385... | collective-permute-start | bytes 2359304 | tf_op jit(solution)/shard_map/ppermute | solution.py:12
  91.5 20.1 %collective-permute-start.2 = (bf16[512,768]{1,0:T(8,128)(2,1)}, bf16[512,768]{1,0:T(8,128)(2,1)S(1)}, u32[]{:S(2)}, u32[]{:S(2)}) collective-permute-start(bf16[512,768]{1,0:T(8,128)(2,1)} %collective-permute-done.1), channel_id=1, source_target_pairs={{0,128},{128,0},{256,384},{384,256},{1,129},{129,1},{257,385},{385... | collective-permute-start | bytes 2359304 | tf_op jit(solution)/shard_map/ppermute | solution.py:12
  93.4 18.5 %collective-permute-start.5 = (bf16[512,768]{1,0:T(8,128)(2,1)}, bf16[512,768]{1,0:T(8,128)(2,1)S(1)}, u32[]{:S(2)}, u32[]{:S(2)}) collective-permute-start(bf16[512,768]{1,0:T(8,128)(2,1)} %collective-permute-done.4), channel_id=1, source_target_pairs={{0,128},{128,0},{256,384},{384,256},{1,129},{129,1},{257,385},{385... | collective-permute-start | bytes 2359304 | tf_op jit(solution)/shard_map/ppermute | solution.py:12
  101.3 14.1 %collective-permute-start.8 = (bf16[512,768]{1,0:T(8,128)(2,1)}, bf16[512,768]{1,0:T(8,128)(2,1)S(1)}, u32[]{:S(2)}, u32[]{:S(2)}) collective-permute-start(bf16[512,768]{1,0:T(8,128)(2,1)} %collective-permute-done.7), channel_id=1, source_target_pairs={{0,128},{128,0},{256,384},{384,256},{1,129},{129,1},{257,385},{385... | collective-permute-start | bytes 2359304 | tf_op jit(solution)/shard_map/ppermute | solution.py:12
  118.8 18.4 %copy-start.3 = (s32[128,2]{0,1:T(2,128)S(1)}, s32[128,2]{0,1:T(2,128)}, u32[]{:S(2)}) copy-start(s32[128,2]{0,1:T(2,128)} %param.11) | copy-start | bytes 3076
  118.8 18.4 %copy-start.6 = (s32[128]{0:T(128)S(1)}, s32[128]{0:T(128)}, u32[]{:S(2)}) copy-start(s32[128]{0:T(128)} %param.14) | copy-start | bytes 1540
  118.8 18.5 %copy-start.5 = (f32[128,2]{0,1:T(2,128)S(1)}, f32[128,2]{0,1:T(2,128)}, u32[]{:S(2)}) copy-start(f32[128,2]{0,1:T(2,128)} %param.12) | copy-start | bytes 3076
  118.8 68.7 %all-to-all-start.1 = ((bf16[128,2,2048]{2,1,0:T(2,128)(2,1)}), bf16[128,2,2048]{2,1,0:T(2,128)(2,1)S(1)}, u32[]{:S(2)}, u32[]{:S(2)}) async-start(bf16[128,2,2048]{2,1,0:T(2,128)(2,1)} %pad_maximum_fusion.1), calls=%async_computation.1 | async-start | bytes 2097152 | tf_op jit(solution)/shard_map/all_to_all | solution.py:57
  190.9 63.4 %all-to-all-start.2 = ((bf16[128,2,2048]{2,1,0:T(2,128)(2,1)}), bf16[128,2,2048]{2,1,0:T(2,128)(2,1)S(1)}, u32[]{:S(2)}, u32[]{:S(2)}) async-start(bf16[128,2,2048]{2,1,0:T(2,128)(2,1)} %reshape.52), calls=%async_computation.2 | async-start | bytes 2097152 | tf_op jit(solution)/shard_map/all_to_all | solution.py:57
  203.9 72.6 %all-gather.2.cloned.1.call-start = ((), (), s32[]{:S(2)}) async-start(), calls=%async_computation.4 | async-start | bytes 1966080 | tf_op jit(solution)/shard_map/all_gather | solution.py:95
  204.0 15.3 %collective-permute-start.11 = (bf16[256,768]{1,0:T(8,128)(2,1)S(1)}, bf16[256,768]{1,0:T(8,128)(2,1)S(1)}, u32[]{:S(2)}, u32[]{:S(2)}) collective-permute-start(bf16[256,768]{1,0:T(8,128)(2,1)S(1)} %multiply_convert_fusion), channel_id=1, source_target_pairs={{0,64},{1,65},{2,66},{3,67},{4,68},{5,69},{6,70},{7,71},{8,72},{9,... | collective-permute-start | bytes 1179656 | tf_op jit(solution)/shard_map/ppermute | solution.py:12
  208.3 21.1 %collective-permute-start.12 = (bf16[256,768]{1,0:T(8,128)(2,1)S(1)}, bf16[256,768]{1,0:T(8,128)(2,1)S(1)}, u32[]{:S(2)}, u32[]{:S(2)}) collective-permute-start(bf16[256,768]{1,0:T(8,128)(2,1)S(1)} %multiply_convert_fusion), channel_id=1, source_target_pairs={{0,32},{1,33},{2,34},{3,35},{4,36},{5,37},{6,38},{7,39},{8,40},{9,... | collective-permute-start | bytes 1179656 | tf_op jit(solution)/shard_map/ppermute | solution.py:12
  256.2 21.7 %all-to-all-start.3 = ((bf16[256,4,512]{2,0,1:T(8,128)(2,1)}), bf16[256,4,512]{2,0,1:T(8,128)(2,1)S(1)}, u32[]{:S(2)}, u32[]{:S(2)}) async-start(bf16[256,4,512]{2,0,1:T(8,128)(2,1)} %copy.17), calls=%async_computation.3 | async-start | bytes 2097152 | tf_op jit(solution)/shard_map/all_to_all | solution.py:120
  264.3 39.8 %collective-permute-start.9 = (bf16[512,768]{1,0:T(8,128)(2,1)}, bf16[512,768]{1,0:T(8,128)(2,1)S(1)}, u32[]{:S(2)}, u32[]{:S(2)}) collective-permute-start(bf16[512,768]{1,0:T(8,128)(2,1)} %bitcast.13), channel_id=1, source_target_pairs={{0,64},{1,65},{2,66},{3,67},{4,68},{5,69},{6,70},{7,71},{8,72},{9,... | collective-permute-start | bytes 2359304 | tf_op jit(solution)/shard_map/ppermute | solution.py:12
  268.9 35.3 %collective-permute-start.10 = (bf16[512,768]{1,0:T(8,128)(2,1)}, bf16[512,768]{1,0:T(8,128)(2,1)S(1)}, u32[]{:S(2)}, u32[]{:S(2)}) collective-permute-start(bf16[512,768]{1,0:T(8,128)(2,1)} %bitcast.13), channel_id=1, source_target_pairs={{0,32},{1,33},{2,34},{3,35},{4,36},{5,37},{6,38},{7,39},{8,40},{9,... | collective-permute-start | bytes 2359304 | tf_op jit(solution)/shard_map/ppermute | solution.py:12
  271.3 32.2 %collective-permute-start.13 = (bf16[512]{0:T(512)(128)(2,1)S(1)}, bf16[512]{0:T(512)(128)(2,1)S(1)}, u32[]{:S(2)}, u32[]{:S(2)}) collective-permute-start(bf16[512]{0:T(512)(128)(2,1)S(1)} %reduce), channel_id=1, source_target_pairs={{0,64},{1,65},{2,66},{3,67},{4,68},{5,69},{6,70},{7,71},{8,72},{9,... | collective-permute-start | bytes 3080 | tf_op jit(solution)/shard_map/ppermute | solution.py:12
  274.6 29.5 %collective-permute-start.14 = (bf16[512]{0:T(512)(128)(2,1)S(1)}, bf16[512]{0:T(512)(128)(2,1)S(1)}, u32[]{:S(2)}, u32[]{:S(2)}) collective-permute-start(bf16[512]{0:T(512)(128)(2,1)S(1)} %reduce), channel_id=1, source_target_pairs={{0,32},{1,33},{2,34},{3,35},{4,36},{5,37},{6,38},{7,39},{8,40},{9,... | collective-permute-start | bytes 3080 | tf_op jit(solution)/shard_map/ppermute | solution.py:12
  (3 other events, 18.6 us)
Sparse Core Ops, SparseCore 0:
  230.3 34.8 all-gather.1
